TPU v7x, 32 devices: a whole 2x2x4 slice. The times are simulated.
32 devices in a mesh: gx: 4 (over y, x), gy: 4 (over z), gz: 2 (over core).
Axes of the slice: x: 2, y: 2, z: 4, core: 2. Of those that a mesh axis runs over, the one named last changes fastest.
Arguments:
- right_side: float32 [16, 256, 512], P('gz', 'gx', 'gy'), may hold values from -6 to 6
- permeability: float32 [16, 256, 512], P('gz', 'gx', 'gy'), may hold values from 0.05 to 50
- storage: float32 [16, 256, 512], P('gz', 'gx', 'gy'), may hold values from 0.05 to 0.5
- deflation: float32 [8, 16, 256, 512], P(None, 'gz', 'gx', 'gy'), may hold values from -0.0234375 to 0.0234375
- coarse_inverse: float32 [256, 256], P('gx'), as said below
- owners: int32 [2, 4, 4, 8], P('gz', 'gx', 'gy'), may hold values from 0 to 255, as said below
- margin: int32 [2, 4, 4, 6], P('gz', 'gx', 'gy'), may hold values from 0 to 1
Outputs:
- solution: float32 [16, 256, 512], P('gz', 'gx', 'gy')
- residual: float32 [16, 256, 512], P('gz', 'gx', 'gy')
Inputs may be any that keep to these rules, and one draw needn't show every extreme that they name: `coarse_inverse`: symmetric and positive definite. `owners`: every coarse index appears exactly once.
All inputs are finite; a program needn't handle non-finite values.
Results may differ from a plain program's by a relative error of at most 0.0003.
Values sent between devices are 32-bit elements; how exact they have to be, the bound alone decides.
No kernel may reach another device: no remote copies, remote signals or barrier semaphores. Data moves between devices by JAX's collectives and lax.ppermute only.
A program may use at most 128 MiB of HBM per device.

v0:
```python
import jax
import jax.numpy as jnp
from jax import lax
from jax.sharding import PartitionSpec as P

ITERS = 4
RELAXATION = 0.7
PRECISE = lax.Precision.HIGHEST


def padded_2(cells, sides, width):
    for axis, dim in sides:
        count = lax.axis_size(axis)
        ends = count - 1
        head = lax.slice_in_dim(cells, 0, width, axis=dim)
        tail = lax.slice_in_dim(cells, cells.shape[dim] - width, cells.shape[dim], axis=dim)
        cells = jnp.concatenate(
            [
                lax.ppermute(tail, axis, [(i, (i + 1) % count) for i in range(ends)]),
                cells,
                lax.ppermute(head, axis, [((i + 1) % count, i) for i in range(ends)]),
            ],
            axis=dim,
        )
    return cells


def conduct(first_perm, second_perm):
    return 2.0 * first_perm * second_perm / jnp.maximum(first_perm + second_perm, 0.05)


def neighbour(padded, dimension, offset):
    starts = [1, 1, 1]
    starts[dimension] = 1 + offset
    limits = [
        starts[0] + padded.shape[0] - 2,
        starts[1] + padded.shape[1] - 2,
        starts[2] + padded.shape[2] - 2,
    ]
    return lax.slice(padded, starts, limits)


def diagonal_of(perm_pad, storage_in):
    perm_center = neighbour(perm_pad, 0, 0)
    diagonal = storage_in
    for dimension in range(3):
        for offset in (-1, 1):
            diagonal = diagonal + conduct(perm_center, neighbour(perm_pad, dimension, offset))
    return diagonal


def stencil(padded, perm_pad, storage_in):
    center = neighbour(padded, 0, 0)
    perm_center = neighbour(perm_pad, 0, 0)
    applied = storage_in * center
    for dimension in range(3):
        for offset in (-1, 1):
            transmit = conduct(perm_center, neighbour(perm_pad, dimension, offset))
            applied = applied + transmit * (center - neighbour(padded, dimension, offset))
    return applied


def line_mask(length, low_side, high_side, position, blocks):
    places = jnp.arange(length + 2, dtype=jnp.int32)
    inside = (places >= 1 - low_side) & (places <= length + high_side)
    ingrid = ((places >= 1) | (position > 0)) & ((places <= length) | (position < blocks - 1))
    return (inside & ingrid).astype(jnp.float32)


def local_solve(residual_ext, perm_pad, storage_ext, keep_mask, inverse):
    source = keep_mask * residual_ext
    solved = RELAXATION * inverse * source
    applied = stencil(jnp.pad(solved, 1), perm_pad, storage_ext)
    solved = solved + RELAXATION * inverse * (source - applied)
    return solved[1:-1, 1:-1, 1:-1]


def local(right_side, permeability, storage, deflation, coarse_inverse, owners, margin):
    widened = padded_2(jnp.stack((permeability, storage)), (("gx", 2), ("gy", 3), ("gz", 1)), 2)
    perm_wide = widened[0]
    perm_near = perm_wide[1:-1, 1:-1, 1:-1]
    storage_ext = widened[1][1:-1, 1:-1, 1:-1]
    local_z, local_x, local_y = right_side.shape
    depths = margin.reshape(6)
    keep_mask = (
        line_mask(local_z, depths[0], depths[1], lax.axis_index("gz"), lax.axis_size("gz"))[
            :, None, None
        ]
        * line_mask(local_x, depths[2], depths[3], lax.axis_index("gx"), lax.axis_size("gx"))[
            None, :, None
        ]
        * line_mask(local_y, depths[4], depths[5], lax.axis_index("gy"), lax.axis_size("gy"))[
            None, None, :
        ]
    )
    diagonal = diagonal_of(perm_wide, storage_ext)
    inverse = keep_mask / jnp.where(keep_mask > 0, diagonal, 1.0)
    flat_vectors = deflation.reshape(deflation.shape[0], -1)
    order_total = coarse_inverse.shape[1]
    owner_list = owners.reshape(-1)
    picker = (owner_list[:, None] == jnp.arange(order_total, dtype=jnp.int32)[None, :]).astype(
        jnp.float32
    )

    def coarse_terms(field):
        coefficients = jnp.dot(flat_vectors, field.reshape(-1), precision=PRECISE)
        return jnp.dot(coefficients, picker, precision=PRECISE)

    def coarse_field(vector):
        solved_part = jnp.dot(coarse_inverse, vector, precision=PRECISE)
        solved = lax.all_gather(solved_part, "gx", axis=0, tiled=True)
        picked = jnp.dot(picker, solved, precision=PRECISE)
        return jnp.dot(picked, flat_vectors, precision=PRECISE).reshape(right_side.shape)

    def residual_rim(residual):
        return padded_2(residual, (("gx", 1), ("gy", 2), ("gz", 0)), 1)

    def precondition(residual_ext, vector):
        return local_solve(residual_ext, perm_wide, storage_ext, keep_mask, inverse) + coarse_field(
            vector
        )

    def inner_of(residual, precond):
        return lax.psum(jnp.sum(residual * precond), ("gx", "gy", "gz"))

    solution = jnp.zeros(right_side.shape, jnp.float32)
    residual = right_side
    residual_ext = residual_rim(residual)
    vector = lax.psum(coarse_terms(residual), ("gx", "gy", "gz"))
    precond = precondition(residual_ext, vector)
    inner_prod = inner_of(residual, precond)
    direction = precond
    for iteration in range(ITERS):
        padded = padded_2(direction, (("gx", 1), ("gy", 2), ("gz", 0)), 1)
        applied = stencil(padded, perm_near, storage)
        curvature, coarse_image = lax.psum(
            (jnp.sum(direction * applied), coarse_terms(applied)), ("gx", "gy", "gz")
        )
        step_size = inner_prod / curvature
        solution = solution + step_size * direction
        residual = residual - step_size * applied
        if iteration + 1 < ITERS:
            residual_ext = residual_rim(residual)
            vector = vector - step_size * coarse_image
            precond = precondition(residual_ext, vector)
            fresh_prod = inner_of(residual, precond)
            direction = precond + fresh_prod / inner_prod * direction
            inner_prod = fresh_prod
    return (solution, residual)


def solution(mesh):
    in_specs = (
        P("gz", "gx", "gy"),
        P("gz", "gx", "gy"),
        P("gz", "gx", "gy"),
        P(None, "gz", "gx", "gy"),
        P("gx", None),
        P("gz", "gx", "gy", None),
        P("gz", "gx", "gy", None),
    )
    out_specs = (P("gz", "gx", "gy"), P("gz", "gx", "gy"))
    return jax.shard_map(local, mesh=mesh, in_specs=in_specs, out_specs=out_specs, check_vma=False)
```

profile of v0, /device:TPU:0, one launch (start us, length us, event | category | flops | bytes accessed | tf_op | source)
XLA Modules:
  0.0 727.6 jit_solution(15111064473556556727)
XLA Ops:
  2.1 4.9 collective-permute-start
  8.3 4.5 collective-permute-start.6
  16.8 6.5 fusion.8
  23.5 42.0 %psum.84 = f32[256]{0:T(256)S(1)} all-reduce(f32[256]{0:T(256)S(1)} %bitcast.151), channel_id=1, replica_groups=mesh['gx'=4,'gy'=4,'gz'=2] {'gx','gy','gz'}, use_global_device_ids=true, to_apply=%region_0.1 | all-reduce | flops 256 | bytes 2048 | tf_op jit(solution)/shard_map/psum | solution.py:129
  67.2 11.1 %all-reduce.4 = f32[256]{0:T(256)S(1)} all-reduce(f32[256]{0:T(256)S(1)} %dynamic-update-slice), channel_id=1, replica_groups=mesh['gx'=4,'gy'=4,'gz'=2] {'gx'}, use_global_device_ids=true, to_apply=%add.4 | all-reduce | flops 256 | bytes 2048
  78.5 2.8 copy.102
  84.0 2.5 fusion.174
  87.6 4.1 collective-permute-start.8
  95.5 5.1 collective-permute-start.2
  114.5 3.8 collective-permute-start.4
  119.9 2.7 multiply_multiply_fusion.3
  123.9 6.1 fusion.144
  130.0 8.2 %multiply_add_fusion.3 = (f32[10,66,130]{2,0,1:T(8,128)}, f32[10,66,130]{2,0,1:T(8,128)}, f32[10,66,130]{2,0,1:T(8,128)}, f32[10,66,130]{2,0,1:T(8,128)}) fusion(f32[10,66,130]{2,0,1:T(8,128)} %get-tuple-element.38, f32[10,66,130]{2,0,1:T(8,128)} %get-tuple-element.34, f32[10,66,130]{2,0,1:T(8,128)} %get-tuple-element.37, ...), kind=kLoop, calls=%fused_computation.57 | loop fusion | flops 1115400 | bytes 3432000 | tf_op jit(solution)/shard_map/add | solution.py:59
  138.2 4.5 fusion.125
  145.4 4.8 collective-permute-done.13
  150.4 4.6 collective-permute-start.14
  156.2 4.7 collective-permute-done.14
  160.9 4.1 collective-permute-done.15
  170.1 2.9 multiply_reduce_fusion.6
  173.1 5.2 fusion.11
  178.5 39.4 %all-reduce.10 = (f32[]{:T(128)}, f32[]{:T(128)}, f32[256]{0:T(256)}) all-reduce(f32[]{:T(128)} %get-tuple-element.7, f32[]{:T(128)} %get-tuple-element.6, f32[256]{0:T(256)S(1)} %bitcast.150), channel_id=1, replica_groups=mesh['gx'=4,'gy'=4,'gz'=2] {'gx','gy','gz'}, use_global_device_ids=true, to_apply=%region_2.3 | all-reduce | flops 258 | bytes 2064 | tf_op jit(solution)/shard_map/psum | solution.py:124
  221.1 4.2 collective-permute-start.18
  230.0 12.2 %all-reduce.5 = f32[256]{0:T(256)} all-reduce(f32[256]{0:T(256)} %dynamic-update-slice.1), channel_id=1, replica_groups=mesh['gx'=4,'gy'=4,'gz'=2] {'gx'}, use_global_device_ids=true, to_apply=%add.5 | all-reduce | flops 256 | bytes 2048
  242.3 3.5 collective-permute-start.20
  249.8 4.4 collective-permute-done.21
  261.4 7.9 %multiply_add_fusion.2 = (f32[10,66,130]{2,0,1:T(8,128)}, f32[10,66,130]{2,0,1:T(8,128)}, f32[10,66,130]{2,0,1:T(8,128)}, f32[10,66,130]{2,0,1:T(8,128)}) fusion(f32[10,66,130]{2,0,1:T(8,128)} %get-tuple-element.38, f32[10,66,130]{2,0,1:T(8,128)} %get-tuple-element.67, f32[10,66,130]{2,0,1:T(8,128)S(1)} %copy-done.8, f32[10,66,130]{2,0,1:T(8,128)S(1)} %copy-done.5, ...), kind=kLoop, calls=%fused_computation.49 | loop fusion | flops 1115400 | bytes 3432000 | tf_op jit(solution)/shard_map/add | solution.py:59
  269.3 5.9 multiply_reduce_fusion.5
  275.1 38.5 %psum.88 = f32[]{:T(128)} all-reduce(f32[]{:T(128)} %get-tuple-element.25), channel_id=1, replica_groups=mesh['gx'=4,'gy'=4,'gz'=2] {'gx','gy','gz'}, use_global_device_ids=true, to_apply=%region_7.8 | all-reduce | flops 1 | bytes 8 | tf_op jit(solution)/shard_map/psum | solution.py:124
  316.0 4.2 collective-permute-start.24
  321.5 4.2 collective-permute-done.25
  326.0 3.4 collective-permute-start.26
  330.7 2.6 collective-permute-done.26
  333.3 4.4 collective-permute-done.27
  344.3 5.2 fusion.14
  350.3 39.3 %all-reduce.9 = (f32[]{:T(128)}, f32[256]{0:T(256)}) all-reduce(f32[]{:T(128)} %get-tuple-element.23, f32[256]{0:T(256)} %bitcast.161), channel_id=1, replica_groups=mesh['gx'=4,'gy'=4,'gz'=2] {'gx','gy','gz'}, use_global_device_ids=true, to_apply=%region_9.10 | all-reduce | flops 257 | bytes 2056 | tf_op jit(solution)/shard_map/psum | solution.py:136
  393.3 4.2 collective-permute-start.30
  401.9 11.7 %all-reduce.6 = f32[256]{0:T(256)S(1)} all-reduce(f32[256]{0:T(256)} %dynamic-update-slice.2), channel_id=1, replica_groups=mesh['gx'=4,'gy'=4,'gz'=2] {'gx'}, use_global_device_ids=true, to_apply=%add.6 | all-reduce | flops 256 | bytes 2048
  414.9 3.3 collective-permute-start.32
  422.1 4.4 collective-permute-done.33
  429.8 2.5 fusion.176
  434.4 7.9 %multiply_add_fusion.1 = (f32[10,66,130]{2,0,1:T(8,128)}, f32[10,66,130]{2,0,1:T(8,128)}, f32[10,66,130]{2,0,1:T(8,128)}, f32[10,66,130]{2,0,1:T(8,128)}) fusion(f32[10,66,130]{2,0,1:T(8,128)} %get-tuple-element.38, f32[10,66,130]{2,0,1:T(8,128)} %get-tuple-element.65, f32[10,66,130]{2,0,1:T(8,128)S(1)} %copy-done.9, f32[10,66,130]{2,0,1:T(8,128)S(1)} %copy-done.6, ...), kind=kLoop, calls=%fused_computation.41 | loop fusion | flops 1115400 | bytes 3432000 | tf_op jit(solution)/shard_map/add | solution.py:59
  442.3 5.9 multiply_reduce_fusion.3
  448.1 38.5 %psum.91 = f32[]{:T(128)} all-reduce(f32[]{:T(128)} %get-tuple-element.21), channel_id=1, replica_groups=mesh['gx'=4,'gy'=4,'gz'=2] {'gx','gy','gz'}, use_global_device_ids=true, to_apply=%region_12.13 | all-reduce | flops 1 | bytes 8 | tf_op jit(solution)/shard_map/psum | solution.py:124
  488.9 4.4 collective-permute-start.36
  494.6 4.2 collective-permute-done.37
  499.0 3.4 collective-permute-start.38
  503.7 2.6 collective-permute-done.38
  506.4 4.4 collective-permute-done.39
  517.2 5.2 fusion.17
  523.2 39.3 %all-reduce.8 = (f32[]{:T(128)}, f32[256]{0:T(256)}) all-reduce(f32[]{:T(128)} %get-tuple-element.19, f32[256]{0:T(256)} %bitcast.162), channel_id=1, replica_groups=mesh['gx'=4,'gy'=4,'gz'=2] {'gx','gy','gz'}, use_global_device_ids=true, to_apply=%region_14.15 | all-reduce | flops 257 | bytes 2056 | tf_op jit(solution)/shard_map/psum | solution.py:136
  566.1 4.2 collective-permute-start.42
  574.3 11.7 %all-reduce.7 = f32[256]{0:T(256)S(1)} all-reduce(f32[256]{0:T(256)} %dynamic-update-slice.3), channel_id=1, replica_groups=mesh['gx'=4,'gy'=4,'gz'=2] {'gx'}, use_global_device_ids=true, to_apply=%add.7 | all-reduce | flops 256 | bytes 2048
  587.2 3.3 collective-permute-start.44
  594.4 4.4 collective-permute-done.45
  602.4 2.5 fusion.177
  607.1 4.5 multiply_add_fusion
  611.7 4.7 multiply_reduce_fusion.1
  616.4 38.4 %psum.94 = f32[]{:T(128)} all-reduce(f32[]{:T(128)} %get-tuple-element.17), channel_id=1, replica_groups=mesh['gx'=4,'gy'=4,'gz'=2] {'gx','gy','gz'}, use_global_device_ids=true, to_apply=%region_17.18 | all-reduce | flops 1 | bytes 8 | tf_op jit(solution)/shard_map/psum | solution.py:124
  656.2 4.2 collective-permute-start.48
  661.7 4.2 collective-permute-done.49
  666.2 3.4 collective-permute-start.50
  670.9 2.6 collective-permute-done.50
  673.5 4.4 collective-permute-done.51
  685.0 39.2 %psum.95 = f32[]{:T(128)} all-reduce(f32[]{:T(128)} %get-tuple-element.15), channel_id=1, replica_groups=mesh['gx'=4,'gy'=4,'gz'=2] {'gx','gy','gz'}, use_global_device_ids=true, to_apply=%region_19.20 | all-reduce | flops 1 | bytes 8 | tf_op jit(solution)/shard_map/psum | solution.py:136
  (308 shorter events, 123.0 us)
Async XLA Ops:
  0.6 64.9 %copy-start = (f32[64,256]{1,0:T(8,128)S(1)}, f32[64,256]{1,0:T(8,128)}, u32[]{:S(2)}) copy-start(f32[64,256]{1,0:T(8,128)} %param.11) | copy-start | bytes 196612
  2.1 91.0 %collective-permute-start = (f32[2,8,2,128]{3,1,2,0:T(8,128)S(1)}, f32[2,8,2,128]{3,1,2,0:T(8,128)S(1)}, u32[]{:S(2)}, u32[]{:S(2)}) collective-permute-start(f32[2,8,2,128]{3,1,2,0:T(8,128)S(1)} %get-tuple-element.86), channel_id=1, source_target_pairs={{0,8},{8,16},{16,24},{1,9},{9,17},{17,25},{2,10},{10,18},{18,26},{... | collective-permute-start | bytes 49160 | tf_op jit(solution)/shard_map/ppermute | solution.py:19
  6.9 86.1 %collective-permute-start.1 = (f32[2,8,2,128]{3,1,2,0:T(8,128)S(1)}, f32[2,8,2,128]{3,1,2,0:T(8,128)S(1)}, u32[]{:S(2)}, u32[]{:S(2)}) collective-permute-start(f32[2,8,2,128]{3,1,2,0:T(8,128)S(1)} %get-tuple-element.87), channel_id=1, source_target_pairs={{8,0},{16,8},{24,16},{9,1},{17,9},{25,17},{10,2},{18,10},{26,18},{... | collective-permute-start | bytes 49160 | tf_op jit(solution)/shard_map/ppermute | solution.py:21
  8.3 78.2 %collective-permute-start.6 = (f32[8,1,128]{2,0,1:T(8,128)S(1)}, f32[8,1,128]{2,0,1:T(8,128)S(1)}, u32[]{:S(2)}, u32[]{:S(2)}) collective-permute-start(f32[8,1,128]{2,0,1:T(8,128)S(1)} %copy.93), channel_id=1, source_target_pairs={{0,8},{8,16},{16,24},{1,9},{9,17},{17,25},{2,10},{10,18},{18,26},{... | collective-permute-start | bytes 12296 | tf_op jit(solution)/shard_map/ppermute | solution.py:19
  12.8 73.8 %collective-permute-start.7 = (f32[8,1,128]{2,0,1:T(8,128)S(1)}, f32[8,1,128]{2,0,1:T(8,128)S(1)}, u32[]{:S(2)}, u32[]{:S(2)}) collective-permute-start(f32[8,1,128]{2,0,1:T(8,128)S(1)} %copy.94), channel_id=1, source_target_pairs={{8,0},{16,8},{24,16},{9,1},{17,9},{25,17},{10,2},{18,10},{26,18},{... | collective-permute-start | bytes 12296 | tf_op jit(solution)/shard_map/ppermute | solution.py:21
  16.8 48.9 %copy-start.69 = (u32[32]{0:T(128)S(1)}, u32[32]{0:T(128)}, u32[]{:S(2)}) copy-start(u32[32]{0:T(128)} %constant.65) | copy-start | bytes 388
  87.6 16.3 %collective-permute-start.8 = (f32[8,66,1]{2,0,1:T(8,128)}, f32[8,66,1]{2,0,1:T(8,128)}, u32[]{:S(2)}, u32[]{:S(2)}) collective-permute-start(f32[8,66,1]{2,0,1:T(8,128)} %get-tuple-element.102), channel_id=1, source_target_pairs={{0,2},{2,4},{4,6},{1,3},{3,5},{5,7},{8,10},{10,12},{12,14},{9,11},... | collective-permute-start | bytes 6344 | tf_op jit(solution)/shard_map/ppermute | solution.py:19
  91.7 12.2 %collective-permute-start.9 = (f32[8,66,1]{2,0,1:T(8,128)}, f32[8,66,1]{2,0,1:T(8,128)}, u32[]{:S(2)}, u32[]{:S(2)}) collective-permute-start(f32[8,66,1]{2,0,1:T(8,128)} %get-tuple-element.103), channel_id=1, source_target_pairs={{2,0},{4,2},{6,4},{3,1},{5,3},{7,5},{10,8},{12,10},{14,12},{11,9},... | collective-permute-start | bytes 6344 | tf_op jit(solution)/shard_map/ppermute | solution.py:21
  95.5 13.9 %collective-permute-start.2 = (f32[2,8,68,2]{2,1,3,0:T(8,128)S(1)}, f32[2,8,68,2]{2,1,3,0:T(8,128)}, u32[]{:S(2)}, u32[]{:S(2)}) collective-permute-start(f32[2,8,68,2]{2,1,3,0:T(8,128)S(1)} %copy.24), channel_id=1, source_target_pairs={{0,2},{2,4},{4,6},{1,3},{3,5},{5,7},{8,10},{10,12},{12,14},{9,11},... | collective-permute-start | bytes 26120 | tf_op jit(solution)/shard_map/ppermute | solution.py:19
  102.6 7.9 %collective-permute-start.3 = (f32[2,8,68,2]{2,1,3,0:T(8,128)}, f32[2,8,68,2]{2,1,3,0:T(8,128)}, u32[]{:S(2)}, u32[]{:S(2)}) collective-permute-start(f32[2,8,68,2]{2,1,3,0:T(8,128)} %copy.25), channel_id=1, source_target_pairs={{2,0},{4,2},{6,4},{3,1},{5,3},{7,5},{10,8},{12,10},{14,12},{11,9},... | collective-permute-start | bytes 26120 | tf_op jit(solution)/shard_map/ppermute | solution.py:21
  106.3 13.6 %collective-permute-start.10 = (f32[1,66,130]{2,0,1:T(1,128)}, f32[1,66,130]{2,0,1:T(1,128)}, u32[]{:S(2)}, u32[]{:S(2)}) collective-permute-start(f32[1,66,130]{2,0,1:T(1,128)} %get-tuple-element.82), channel_id=1, source_target_pairs={{0,1},{2,3},{4,5},{6,7},{8,9},{10,11},{12,13},{14,15},{16,17},{18,... | collective-permute-start | bytes 102968 | tf_op jit(solution)/shard_map/ppermute | solution.py:19
  108.2 11.7 %collective-permute-start.11 = (f32[1,66,130]{2,0,1:T(1,128)}, f32[1,66,130]{2,0,1:T(1,128)}, u32[]{:S(2)}, u32[]{:S(2)}) collective-permute-start(f32[1,66,130]{2,0,1:T(1,128)} %get-tuple-element.83), channel_id=1, source_target_pairs={{1,0},{3,2},{5,4},{7,6},{9,8},{11,10},{13,12},{15,14},{17,16},{19,... | collective-permute-start | bytes 102968 | tf_op jit(solution)/shard_map/ppermute | solution.py:21
  114.5 8.1 %collective-permute-start.4 = (f32[2,2,68,132]{3,1,2,0:T(2,128)S(1)}, f32[2,2,68,132]{3,1,2,0:T(2,128)S(1)}, u32[]{:S(2)}, u32[]{:S(2)}) collective-permute-start(f32[2,2,68,132]{3,1,2,0:T(2,128)S(1)} %get-tuple-element.44), channel_id=1, source_target_pairs={{0,1},{2,3},{4,5},{6,7},{8,9},{10,11},{12,13},{14,15},{16,17},{18,... | collective-permute-start | bytes 430856 | tf_op jit(solution)/shard_map/ppermute | solution.py:19
  118.3 4.3 collective-permute-start.5
  142.7 27.4 %copy-start.17 = (f32[8,64,128]{2,0,1:T(8,128)}, f32[8,64,128]{2,0,1:T(8,128)S(1)}, u32[]{:S(2)}) copy-start(f32[8,64,128]{2,0,1:T(8,128)S(1)} %fusion.125) | copy-start | bytes 786436
  142.7 2.6 collective-permute-start.12
  144.0 6.1 collective-permute-start.13
  150.2 19.9 %copy-start.25 = (f32[8,64,128]{2,1,0:T(8,128)S(1)}, f32[8,64,128]{2,1,0:T(8,128)}, u32[]{:S(2)}) copy-start(f32[8,64,128]{2,1,0:T(8,128)} %param.9) | copy-start | bytes 786436
  150.4 10.6 %collective-permute-start.14 = (f32[8,66,1]{2,0,1:T(8,128)S(1)}, f32[8,66,1]{2,0,1:T(8,128)S(1)}, u32[]{:S(2)}, u32[]{:S(2)}) collective-permute-start(f32[8,66,1]{2,0,1:T(8,128)S(1)} %get-tuple-element.100), channel_id=1, source_target_pairs={{0,2},{2,4},{4,6},{1,3},{3,5},{5,7},{8,10},{10,12},{12,14},{9,11},... | collective-permute-start | bytes 6344 | tf_op jit(solution)/shard_map/ppermute | solution.py:19
  154.9 10.1 %collective-permute-start.15 = (f32[8,66,1]{2,0,1:T(8,128)S(1)}, f32[8,66,1]{2,0,1:T(8,128)S(1)}, u32[]{:S(2)}, u32[]{:S(2)}) collective-permute-start(f32[8,66,1]{2,0,1:T(8,128)S(1)} %get-tuple-element.101), channel_id=1, source_target_pairs={{2,0},{4,2},{6,4},{3,1},{5,3},{7,5},{10,8},{12,10},{14,12},{11,9},... | collective-permute-start | bytes 6344 | tf_op jit(solution)/shard_map/ppermute | solution.py:21
  165.5 2.7 collective-permute-start.16
  166.9 3.3 collective-permute-start.17
  220.5 48.8 %copy-start.22 = (f32[8,64,128]{2,0,1:T(8,128)}, f32[8,64,128]{2,0,1:T(8,128)S(1)}, u32[]{:S(2)}) copy-start(f32[8,64,128]{2,0,1:T(8,128)S(1)} %multiply_subtract_fusion.3) | copy-start | bytes 786436
  221.1 21.0 %collective-permute-start.18 = (f32[8,1,128]{2,0,1:T(8,128)}, f32[8,1,128]{2,0,1:T(8,128)S(1)}, u32[]{:S(2)}, u32[]{:S(2)}) collective-permute-start(f32[8,1,128]{2,0,1:T(8,128)} %get-tuple-element.114), channel_id=1, source_target_pairs={{0,8},{8,16},{16,24},{1,9},{9,17},{17,25},{2,10},{10,18},{18,26},{... | collective-permute-start | bytes 12296 | tf_op jit(solution)/shard_map/ppermute | solution.py:19
  225.3 16.8 %collective-permute-start.19 = (f32[8,1,128]{2,0,1:T(8,128)}, f32[8,1,128]{2,0,1:T(8,128)S(1)}, u32[]{:S(2)}, u32[]{:S(2)}) collective-permute-start(f32[8,1,128]{2,0,1:T(8,128)} %get-tuple-element.115), channel_id=1, source_target_pairs={{8,0},{16,8},{24,16},{9,1},{17,9},{25,17},{10,2},{18,10},{26,18},{... | collective-permute-start | bytes 12296 | tf_op jit(solution)/shard_map/ppermute | solution.py:21
  242.3 7.5 %collective-permute-start.20 = (f32[8,66,1]{2,0,1:T(8,128)S(1)}, f32[8,66,1]{2,0,1:T(8,128)S(1)}, u32[]{:S(2)}, u32[]{:S(2)}) collective-permute-start(f32[8,66,1]{2,0,1:T(8,128)S(1)} %get-tuple-element.98), channel_id=1, source_target_pairs={{0,2},{2,4},{4,6},{1,3},{3,5},{5,7},{8,10},{10,12},{12,14},{9,11},... | collective-permute-start | bytes 6344 | tf_op jit(solution)/shard_map/ppermute | solution.py:19
  245.9 8.4 %collective-permute-start.21 = (f32[8,66,1]{2,0,1:T(8,128)S(1)}, f32[8,66,1]{2,0,1:T(8,128)S(1)}, u32[]{:S(2)}, u32[]{:S(2)}) collective-permute-start(f32[8,66,1]{2,0,1:T(8,128)S(1)} %get-tuple-element.99), channel_id=1, source_target_pairs={{2,0},{4,2},{6,4},{3,1},{5,3},{7,5},{10,8},{12,10},{14,12},{11,9},... | collective-permute-start | bytes 6344 | tf_op jit(solution)/shard_map/ppermute | solution.py:21
  254.7 4.6 collective-permute-start.22
  256.0 3.3 collective-permute-start.23
  316.0 5.5 collective-permute-start.24
  320.2 5.5 collective-permute-start.25
  326.0 7.4 %collective-permute-start.26 = (f32[8,66,1]{2,0,1:T(8,128)S(1)}, f32[8,66,1]{2,0,1:T(8,128)S(1)}, u32[]{:S(2)}, u32[]{:S(2)}) collective-permute-start(f32[8,66,1]{2,0,1:T(8,128)S(1)} %get-tuple-element.96), channel_id=1, source_target_pairs={{0,2},{2,4},{4,6},{1,3},{3,5},{5,7},{8,10},{10,12},{12,14},{9,11},... | collective-permute-start | bytes 6344 | tf_op jit(solution)/shard_map/ppermute | solution.py:19
  329.4 8.4 %collective-permute-start.27 = (f32[8,66,1]{2,0,1:T(8,128)S(1)}, f32[8,66,1]{2,0,1:T(8,128)S(1)}, u32[]{:S(2)}, u32[]{:S(2)}) collective-permute-start(f32[8,66,1]{2,0,1:T(8,128)S(1)} %get-tuple-element.97), channel_id=1, source_target_pairs={{2,0},{4,2},{6,4},{3,1},{5,3},{7,5},{10,8},{12,10},{14,12},{11,9},... | collective-permute-start | bytes 6344 | tf_op jit(solution)/shard_map/ppermute | solution.py:21
  338.2 2.8 collective-permute-start.28
  339.5 3.2 collective-permute-start.29
  393.3 20.4 %collective-permute-start.30 = (f32[8,1,128]{2,0,1:T(8,128)}, f32[8,1,128]{2,0,1:T(8,128)S(1)}, u32[]{:S(2)}, u32[]{:S(2)}) collective-permute-start(f32[8,1,128]{2,0,1:T(8,128)} %get-tuple-element.110), channel_id=1, source_target_pairs={{0,8},{8,16},{16,24},{1,9},{9,17},{17,25},{2,10},{10,18},{18,26},{... | collective-permute-start | bytes 12296 | tf_op jit(solution)/shard_map/ppermute | solution.py:19
  397.4 16.3 %collective-permute-start.31 = (f32[8,1,128]{2,0,1:T(8,128)}, f32[8,1,128]{2,0,1:T(8,128)S(1)}, u32[]{:S(2)}, u32[]{:S(2)}) collective-permute-start(f32[8,1,128]{2,0,1:T(8,128)} %get-tuple-element.111), channel_id=1, source_target_pairs={{8,0},{16,8},{24,16},{9,1},{17,9},{25,17},{10,2},{18,10},{26,18},{... | collective-permute-start | bytes 12296 | tf_op jit(solution)/shard_map/ppermute | solution.py:21
  414.9 7.3 collective-permute-start.32
  418.2 8.4 %collective-permute-start.33 = (f32[8,66,1]{2,0,1:T(8,128)S(1)}, f32[8,66,1]{2,0,1:T(8,128)S(1)}, u32[]{:S(2)}, u32[]{:S(2)}) collective-permute-start(f32[8,66,1]{2,0,1:T(8,128)S(1)} %get-tuple-element.95), channel_id=1, source_target_pairs={{2,0},{4,2},{6,4},{3,1},{5,3},{7,5},{10,8},{12,10},{14,12},{11,9},... | collective-permute-start | bytes 6344 | tf_op jit(solution)/shard_map/ppermute | solution.py:21
  427.0 5.3 collective-permute-start.34
  428.4 3.9 collective-permute-start.35
  488.8 27.0 %copy-start.15 = (f32[8,64,128]{2,0,1:T(8,128)}, f32[8,64,128]{2,0,1:T(8,128)S(1)}, u32[]{:S(2)}) copy-start(f32[8,64,128]{2,0,1:T(8,128)S(1)} %multiply_add_fusion.6) | copy-start | bytes 786436
  488.9 5.7 collective-permute-start.36
  493.3 5.5 collective-permute-start.37
  499.0 7.4 %collective-permute-start.38 = (f32[8,66,1]{2,0,1:T(8,128)S(1)}, f32[8,66,1]{2,0,1:T(8,128)S(1)}, u32[]{:S(2)}, u32[]{:S(2)}) collective-permute-start(f32[8,66,1]{2,0,1:T(8,128)S(1)} %get-tuple-element.92), channel_id=1, source_target_pairs={{0,2},{2,4},{4,6},{1,3},{3,5},{5,7},{8,10},{10,12},{12,14},{9,11},... | collective-permute-start | bytes 6344 | tf_op jit(solution)/shard_map/ppermute | solution.py:19
  502.4 8.4 %collective-permute-start.39 = (f32[8,66,1]{2,0,1:T(8,128)S(1)}, f32[8,66,1]{2,0,1:T(8,128)S(1)}, u32[]{:S(2)}, u32[]{:S(2)}) collective-permute-start(f32[8,66,1]{2,0,1:T(8,128)S(1)} %get-tuple-element.93), channel_id=1, source_target_pairs={{2,0},{4,2},{6,4},{3,1},{5,3},{7,5},{10,8},{12,10},{14,12},{11,9},... | collective-permute-start | bytes 6344 | tf_op jit(solution)/shard_map/ppermute | solution.py:21
  511.3 2.7 collective-permute-start.40
  512.6 3.3 collective-permute-start.41
  517.2 54.3 %copy-start.63 = (f32[256]{0:T(256)S(1)}, f32[256]{0:T(256)}, u32[]{:S(2)}) copy-start(f32[256]{0:T(256)} %copy-done.62) | copy-start | bytes 3076
  566.1 19.9 %collective-permute-start.42 = (f32[8,1,128]{2,0,1:T(8,128)}, f32[8,1,128]{2,0,1:T(8,128)S(1)}, u32[]{:S(2)}, u32[]{:S(2)}) collective-permute-start(f32[8,1,128]{2,0,1:T(8,128)} %get-tuple-element.106), channel_id=1, source_target_pairs={{0,8},{8,16},{16,24},{1,9},{9,17},{17,25},{2,10},{10,18},{18,26},{... | collective-permute-start | bytes 12296 | tf_op jit(solution)/shard_map/ppermute | solution.py:19
  570.2 15.8 %collective-permute-start.43 = (f32[8,1,128]{2,0,1:T(8,128)}, f32[8,1,128]{2,0,1:T(8,128)S(1)}, u32[]{:S(2)}, u32[]{:S(2)}) collective-permute-start(f32[8,1,128]{2,0,1:T(8,128)} %get-tuple-element.107), channel_id=1, source_target_pairs={{8,0},{16,8},{24,16},{9,1},{17,9},{25,17},{10,2},{18,10},{26,18},{... | collective-permute-start | bytes 12296 | tf_op jit(solution)/shard_map/ppermute | solution.py:21
  587.2 7.3 collective-permute-start.44
  590.5 8.4 %collective-permute-start.45 = (f32[8,66,1]{2,0,1:T(8,128)S(1)}, f32[8,66,1]{2,0,1:T(8,128)S(1)}, u32[]{:S(2)}, u32[]{:S(2)}) collective-permute-start(f32[8,66,1]{2,0,1:T(8,128)S(1)} %get-tuple-element.91), channel_id=1, source_target_pairs={{2,0},{4,2},{6,4},{3,1},{5,3},{7,5},{10,8},{12,10},{14,12},{11,9},... | collective-permute-start | bytes 6344 | tf_op jit(solution)/shard_map/ppermute | solution.py:21
  599.4 5.5 collective-permute-start.46
  600.7 4.2 collective-permute-start.47
  611.7 44.5 %copy-start.16 = (f32[8,64,128]{2,0,1:T(8,128)S(1)}, f32[8,64,128]{2,0,1:T(8,128)}, u32[]{:S(2)}) copy-start(f32[8,64,128]{2,0,1:T(8,128)} %copy-done.15) | copy-start | bytes 786436
  656.2 5.5 collective-permute-start.48
  660.4 5.5 collective-permute-start.49
  666.2 7.4 %collective-permute-start.50 = (f32[8,66,1]{2,0,1:T(8,128)S(1)}, f32[8,66,1]{2,0,1:T(8,128)S(1)}, u32[]{:S(2)}, u32[]{:S(2)}) collective-permute-start(f32[8,66,1]{2,0,1:T(8,128)S(1)} %get-tuple-element.88), channel_id=1, source_target_pairs={{0,2},{2,4},{4,6},{1,3},{3,5},{5,7},{8,10},{10,12},{12,14},{9,11},... | collective-permute-start | bytes 6344 | tf_op jit(solution)/shard_map/ppermute | solution.py:19
  669.6 8.4 %collective-permute-start.51 = (f32[8,66,1]{2,0,1:T(8,128)S(1)}, f32[8,66,1]{2,0,1:T(8,128)S(1)}, u32[]{:S(2)}, u32[]{:S(2)}) collective-permute-start(f32[8,66,1]{2,0,1:T(8,128)S(1)} %get-tuple-element.89), channel_id=1, source_target_pairs={{2,0},{4,2},{6,4},{3,1},{5,3},{7,5},{10,8},{12,10},{14,12},{11,9},... | collective-permute-start | bytes 6344 | tf_op jit(solution)/shard_map/ppermute | solution.py:21
  678.4 2.7 collective-permute-start.52
  679.8 45.8 %copy-start.18 = (f32[8,64,128]{2,0,1:T(8,128)S(1)}, f32[8,64,128]{2,0,1:T(8,128)}, u32[]{:S(2)}) copy-start(f32[8,64,128]{2,0,1:T(8,128)} %copy-done.17) | copy-start | bytes 786436
  679.8 3.3 collective-permute-start.53
  685.0 40.6 %copy-start.57 = (f32[8,64,128]{2,0,1:T(8,128)S(1)}, f32[8,64,128]{2,0,1:T(8,128)}, u32[]{:S(2)}) copy-start(f32[8,64,128]{2,0,1:T(8,128)} %get-tuple-element.16) | copy-start | bytes 786436
  (60 other events, 579.1 us)
where the time goes:
time: 739 us; the launch traced here: 728 us
  blocking collectives  361 us (49%)
  starting transfers between devices  121 us (16%)
  other arithmetic  90.9 us (12%)
  waiting for transfers between devices  73.3 us (10%)
  matrix products  37.2 us (5%)
  local copies, waits for them, and re-layouts  27.4 us (4%)
  between operations  16.1 us (2%)
    psum x4, blocking collectives, inner_of(): return lax.psum(jnp.sum(residual * precond), ('gx', 'gy', 'gz'))  155 us
    psum x3, blocking collectives, local(): lax.psum((jnp.sum(direction * applied), coarse_terms(applied)), ('gx', 'g...  118 us
    ppermute x27, starting transfers between devices, padded_2(): lax.ppermute(tail, axis, [(i, (i + 1) % count) for i in range(ends)])  85 us
    ppermute x27, waiting for transfers between devices, padded_2(): lax.ppermute(head, axis, [((i + 1) % count, i) for i in range(ends)])  55.2 us
    unnamed x4, blocking collectives  46.7 us
    psum x1, blocking collectives, local(): vector = lax.psum(coarse_terms(residual), ('gx', 'gy', 'gz'))  42 us
    ppermute x27, starting transfers between devices, padded_2(): lax.ppermute(head, axis, [((i + 1) % count, i) for i in range(ends)])  36.3 us
    add x4, other arithmetic, stencil(): applied + transmit * (center - neighbour(padded, dimension, offset))  28.6 us
  transfers between devices with their start and end apart: 54, of which 22 were waited for; matrix products, arithmetic and copies ran while one was open for 7% of the time, Pallas kernels for 0%

commit v1 on v0

--- a/solution.py
+++ b/solution.py
@@ -126,7 +126,7 @@
     solution = jnp.zeros(right_side.shape, jnp.float32)
     residual = right_side
     residual_ext = residual_rim(residual)
-    vector = lax.psum(coarse_terms(residual), ("gx", "gy", "gz"))
+    vector = lax.psum(lax.psum(coarse_terms(residual), ("gy", "gz")), "gx")
     precond = precondition(residual_ext, vector)
     inner_prod = inner_of(residual, precond)
     direction = precond

time: 739 us -> 724 us (0.980)
  blocking collectives: 361 us -> 344 us
    psum x1 -> x2, blocking collectives: 42 us -> 26.5 us  [local(): vector = lax.psum(lax.psum(coarse_terms(residual), ('gy', 'gz')), 'gx')]
where the time goes in v1:
time: 724 us; the launch traced here: 713 us
  blocking collectives  344 us (48%)
  starting transfers between devices  120 us (17%)
  other arithmetic  92.6 us (13%)
  waiting for transfers between devices  72.7 us (10%)
  matrix products  37.4 us (5%)
  local copies, waits for them, and re-layouts  29.2 us (4%)
  between operations  16.7 us (2%)
    psum x4, blocking collectives, inner_of(): return lax.psum(jnp.sum(residual * precond), ('gx', 'gy', 'gz'))  155 us
    psum x3, blocking collectives, local(): lax.psum((jnp.sum(direction * applied), coarse_terms(applied)), ('gx', 'g...  118 us
    ppermute x27, starting transfers between devices, padded_2(): lax.ppermute(tail, axis, [(i, (i + 1) % count) for i in range(ends)])  83.7 us
    ppermute x27, waiting for transfers between devices, padded_2(): lax.ppermute(head, axis, [((i + 1) % count, i) for i in range(ends)])  54.6 us
    unnamed x4, blocking collectives  44.8 us
    ppermute x27, starting transfers between devices, padded_2(): lax.ppermute(head, axis, [((i + 1) % count, i) for i in range(ends)])  36.3 us
    add x4, other arithmetic, stencil(): applied + transmit * (center - neighbour(padded, dimension, offset))  31.4 us
    psum x2, blocking collectives, local(): vector = lax.psum(lax.psum(coarse_terms(residual), ('gy', 'gz')), 'gx')  26.5 us
  transfers between devices with their start and end apart: 54, of which 22 were waited for; matrix products, arithmetic and copies ran while one was open for 7% of the time, Pallas kernels for 0%

profile of v1, /device:TPU:0, one launch (start us, length us, event | category | flops | bytes accessed | tf_op | source)
XLA Modules:
  0.0 712.7 jit_solution(421256332715025427)
XLA Ops:
  2.7 5.5 collective-permute-start
  9.4 4.5 collective-permute-start.6
  17.9 6.5 fusion.8
  24.6 15.8 %psum.91 = f32[256]{0:T(256)S(1)} all-reduce(f32[256]{0:T(256)S(1)} %bitcast.151), channel_id=1, replica_groups=mesh['gx'=4,'gy'=4,'gz'=2] {'gy','gz'}, use_global_device_ids=true, to_apply=%region_0.1 | all-reduce | flops 256 | bytes 2048 | tf_op jit(solution)/shard_map/psum | solution.py:129
  40.4 10.8 %psum.92 = f32[256]{0:T(256)S(1)} all-reduce(f32[256]{0:T(256)S(1)} %psum.91), channel_id=1, replica_groups=mesh['gx'=4,'gy'=4,'gz'=2] {'gx'}, use_global_device_ids=true, to_apply=%region_1.2 | all-reduce | flops 256 | bytes 2048 | tf_op jit(solution)/shard_map/psum | solution.py:129
  52.8 9.2 %all-reduce.4 = f32[256]{0:T(256)S(1)} all-reduce(f32[256]{0:T(256)S(1)} %dynamic-update-slice), channel_id=1, replica_groups=mesh['gx'=4,'gy'=4,'gz'=2] {'gx'}, use_global_device_ids=true, to_apply=%add.4 | all-reduce | flops 256 | bytes 2048
  62.2 2.8 copy.102
  67.1 2.5 fusion.174
  77.1 5.1 collective-permute-start.2
  93.5 2.5 pad_maximum_fusion.7
  96.1 3.8 collective-permute-start.4
  101.4 2.5 multiply_multiply_fusion.3
  106.9 5.7 fusion.144
  112.6 8.2 %multiply_add_fusion.3 = (f32[10,66,130]{2,0,1:T(8,128)}, f32[10,66,130]{2,0,1:T(8,128)}, f32[10,66,130]{2,0,1:T(8,128)}, f32[10,66,130]{2,0,1:T(8,128)}) fusion(f32[10,66,130]{2,0,1:T(8,128)} %get-tuple-element.38, f32[10,66,130]{2,0,1:T(8,128)} %get-tuple-element.34, f32[10,66,130]{2,0,1:T(8,128)S(1)} %get-tuple-element.37, ...), kind=kLoop, calls=%fused_computation.57 | loop fusion | flops 1115400 | bytes 3432000 | tf_op jit(solution)/shard_map/add | solution.py:59
  120.8 4.5 fusion.125
  128.8 4.2 collective-permute-done.13
  133.2 4.6 collective-permute-start.14
  139.1 4.7 collective-permute-done.14
  143.7 4.1 collective-permute-done.15
  152.9 2.9 multiply_reduce_fusion.6
  155.8 5.2 fusion.11
  161.3 39.1 %all-reduce.10 = (f32[]{:T(128)}, f32[]{:T(128)}, f32[256]{0:T(256)}) all-reduce(f32[]{:T(128)} %get-tuple-element.7, f32[]{:T(128)} %get-tuple-element.6, f32[256]{0:T(256)S(1)} %bitcast.150), channel_id=1, replica_groups=mesh['gx'=4,'gy'=4,'gz'=2] {'gx','gy','gz'}, use_global_device_ids=true, to_apply=%region_3.4 | all-reduce | flops 258 | bytes 2064 | tf_op jit(solution)/shard_map/psum | solution.py:124
  203.6 4.2 collective-permute-start.18
  212.2 12.1 %all-reduce.5 = f32[256]{0:T(256)} all-reduce(f32[256]{0:T(256)} %dynamic-update-slice.1), channel_id=1, replica_groups=mesh['gx'=4,'gy'=4,'gz'=2] {'gx'}, use_global_device_ids=true, to_apply=%add.5 | all-reduce | flops 256 | bytes 2048
  224.6 3.7 collective-permute-start.20
  232.2 4.4 collective-permute-done.21
  244.8 7.9 %multiply_add_fusion.2 = (f32[10,66,130]{2,0,1:T(8,128)}, f32[10,66,130]{2,0,1:T(8,128)}, f32[10,66,130]{2,0,1:T(8,128)}, f32[10,66,130]{2,0,1:T(8,128)}) fusion(f32[10,66,130]{2,0,1:T(8,128)S(1)} %copy-done.12, f32[10,66,130]{2,0,1:T(8,128)} %get-tuple-element.67, f32[10,66,130]{2,0,1:T(8,128)S(1)} %copy-done.9, f32[10,66,130]{2,0,1:T(8,128)S(1)} %copy-done.5, ...), kind=kLoop, calls=%fused_computation.49 | loop fusion | flops 1115400 | bytes 3432000 | tf_op jit(solution)/shard_map/add | solution.py:59
  252.7 5.9 multiply_reduce_fusion.5
  258.6 38.5 %psum.96 = f32[]{:T(128)} all-reduce(f32[]{:T(128)} %get-tuple-element.25), channel_id=1, replica_groups=mesh['gx'=4,'gy'=4,'gz'=2] {'gx','gy','gz'}, use_global_device_ids=true, to_apply=%region_8.9 | all-reduce | flops 1 | bytes 8 | tf_op jit(solution)/shard_map/psum | solution.py:124
  299.5 4.2 collective-permute-start.24
  305.0 4.2 collective-permute-done.25
  309.4 3.4 collective-permute-start.26
  314.1 2.6 collective-permute-done.26
  316.8 4.4 collective-permute-done.27
  327.8 5.2 fusion.14
  333.8 39.3 %all-reduce.9 = (f32[]{:T(128)}, f32[256]{0:T(256)}) all-reduce(f32[]{:T(128)} %get-tuple-element.23, f32[256]{0:T(256)} %bitcast.161), channel_id=1, replica_groups=mesh['gx'=4,'gy'=4,'gz'=2] {'gx','gy','gz'}, use_global_device_ids=true, to_apply=%region_10.11 | all-reduce | flops 257 | bytes 2056 | tf_op jit(solution)/shard_map/psum | solution.py:136
  376.8 4.3 collective-permute-start.30
  385.7 11.7 %all-reduce.6 = f32[256]{0:T(256)S(1)} all-reduce(f32[256]{0:T(256)} %dynamic-update-slice.2), channel_id=1, replica_groups=mesh['gx'=4,'gy'=4,'gz'=2] {'gx'}, use_global_device_ids=true, to_apply=%add.6 | all-reduce | flops 256 | bytes 2048
  398.6 3.3 collective-permute-start.32
  405.9 4.4 collective-permute-done.33
  418.4 7.9 %multiply_add_fusion.1 = (f32[10,66,130]{2,0,1:T(8,128)}, f32[10,66,130]{2,0,1:T(8,128)}, f32[10,66,130]{2,0,1:T(8,128)}, f32[10,66,130]{2,0,1:T(8,128)}) fusion(f32[10,66,130]{2,0,1:T(8,128)S(1)} %copy-done.13, f32[10,66,130]{2,0,1:T(8,128)} %get-tuple-element.65, f32[10,66,130]{2,0,1:T(8,128)S(1)} %copy-done.10, f32[10,66,130]{2,0,1:T(8,128)S(1)} %copy-done.6, ...), kind=kLoop, calls=%fused_computation.41 | loop fusion | flops 1115400 | bytes 3432000 | tf_op jit(solution)/shard_map/add | solution.py:59
  426.3 5.9 multiply_reduce_fusion.3
  432.2 38.7 %psum.99 = f32[]{:T(128)} all-reduce(f32[]{:T(128)} %get-tuple-element.21), channel_id=1, replica_groups=mesh['gx'=4,'gy'=4,'gz'=2] {'gx','gy','gz'}, use_global_device_ids=true, to_apply=%region_13.14 | all-reduce | flops 1 | bytes 8 | tf_op jit(solution)/shard_map/psum | solution.py:124
  473.2 4.2 collective-permute-start.36
  478.7 4.2 collective-permute-done.37
  483.1 3.4 collective-permute-start.38
  487.8 2.6 collective-permute-done.38
  490.5 4.4 collective-permute-done.39
  501.4 5.2 fusion.17
  506.8 39.3 %all-reduce.8 = (f32[]{:T(128)}, f32[256]{0:T(256)}) all-reduce(f32[]{:T(128)} %get-tuple-element.19, f32[256]{0:T(256)S(1)} %bitcast.162), channel_id=1, replica_groups=mesh['gx'=4,'gy'=4,'gz'=2] {'gx','gy','gz'}, use_global_device_ids=true, to_apply=%region_15.16 | all-reduce | flops 257 | bytes 2056 | tf_op jit(solution)/shard_map/psum | solution.py:136
  549.2 4.2 collective-permute-start.42
  557.3 11.7 %all-reduce.7 = f32[256]{0:T(256)S(1)} all-reduce(f32[256]{0:T(256)} %dynamic-update-slice.3), channel_id=1, replica_groups=mesh['gx'=4,'gy'=4,'gz'=2] {'gx'}, use_global_device_ids=true, to_apply=%add.7 | all-reduce | flops 256 | bytes 2048
  569.2 3.3 collective-permute-start.44
  576.4 4.4 collective-permute-done.45
  584.4 2.5 fusion.177
  589.3 7.4 %multiply_add_fusion = (f32[10,66,130]{2,0,1:T(8,128)}, f32[10,66,130]{2,0,1:T(8,128)}, f32[10,66,130]{2,0,1:T(8,128)}, f32[10,66,130]{2,0,1:T(8,128)}) fusion(f32[10,66,130]{2,0,1:T(8,128)S(1)} %copy-done.14, f32[10,66,130]{2,0,1:T(8,128)} %get-tuple-element.63, f32[10,66,130]{2,0,1:T(8,128)S(1)} %copy-done.11, f32[10,66,130]{2,0,1:T(8,128)S(1)} %copy-done.7, ...), kind=kLoop, calls=%fused_computation.33 | loop fusion | flops 1115400 | bytes 3432000 | tf_op jit(solution)/shard_map/add | solution.py:59
  596.7 5.1 multiply_reduce_fusion.1
  601.8 38.5 %psum.102 = f32[]{:T(128)} all-reduce(f32[]{:T(128)} %get-tuple-element.17), channel_id=1, replica_groups=mesh['gx'=4,'gy'=4,'gz'=2] {'gx','gy','gz'}, use_global_device_ids=true, to_apply=%region_18.19 | all-reduce | flops 1 | bytes 8 | tf_op jit(solution)/shard_map/psum | solution.py:124
  641.8 4.2 collective-permute-start.48
  647.3 4.2 collective-permute-done.49
  651.7 3.4 collective-permute-start.50
  656.5 2.6 collective-permute-done.50
  659.1 4.4 collective-permute-done.51
  669.9 39.3 %psum.103 = f32[]{:T(128)} all-reduce(f32[]{:T(128)} %get-tuple-element.15), channel_id=1, replica_groups=mesh['gx'=4,'gy'=4,'gz'=2] {'gx','gy','gz'}, use_global_device_ids=true, to_apply=%region_20.21 | all-reduce | flops 1 | bytes 8 | tf_op jit(solution)/shard_map/psum | solution.py:136
  (341 shorter events, 126.2 us)
Async XLA Ops:
  0.6 50.5 %copy-start = (f32[64,256]{1,0:T(8,128)S(1)}, f32[64,256]{1,0:T(8,128)}, u32[]{:S(2)}) copy-start(f32[64,256]{1,0:T(8,128)} %param.11) | copy-start | bytes 196612
  2.7 70.6 %collective-permute-start = (f32[2,8,2,128]{3,1,2,0:T(8,128)}, f32[2,8,2,128]{3,1,2,0:T(8,128)}, u32[]{:S(2)}, u32[]{:S(2)}) collective-permute-start(f32[2,8,2,128]{3,1,2,0:T(8,128)} %get-tuple-element.86), channel_id=1, source_target_pairs={{0,8},{8,16},{16,24},{1,9},{9,17},{17,25},{2,10},{10,18},{18,26},{... | collective-permute-start | bytes 49160 | tf_op jit(solution)/shard_map/ppermute | solution.py:19
  8.1 65.2 %collective-permute-start.1 = (f32[2,8,2,128]{3,1,2,0:T(8,128)}, f32[2,8,2,128]{3,1,2,0:T(8,128)}, u32[]{:S(2)}, u32[]{:S(2)}) collective-permute-start(f32[2,8,2,128]{3,1,2,0:T(8,128)} %get-tuple-element.87), channel_id=1, source_target_pairs={{8,0},{16,8},{24,16},{9,1},{17,9},{25,17},{10,2},{18,10},{26,18},{... | collective-permute-start | bytes 49160 | tf_op jit(solution)/shard_map/ppermute | solution.py:21
  9.4 60.1 %collective-permute-start.6 = (f32[8,1,128]{2,0,1:T(8,128)S(1)}, f32[8,1,128]{2,0,1:T(8,128)S(1)}, u32[]{:S(2)}, u32[]{:S(2)}) collective-permute-start(f32[8,1,128]{2,0,1:T(8,128)S(1)} %copy.93), channel_id=1, source_target_pairs={{0,8},{8,16},{16,24},{1,9},{9,17},{17,25},{2,10},{10,18},{18,26},{... | collective-permute-start | bytes 12296 | tf_op jit(solution)/shard_map/ppermute | solution.py:19
  14.0 55.7 %collective-permute-start.7 = (f32[8,1,128]{2,0,1:T(8,128)S(1)}, f32[8,1,128]{2,0,1:T(8,128)S(1)}, u32[]{:S(2)}, u32[]{:S(2)}) collective-permute-start(f32[8,1,128]{2,0,1:T(8,128)S(1)} %copy.94), channel_id=1, source_target_pairs={{8,0},{16,8},{24,16},{9,1},{17,9},{25,17},{10,2},{18,10},{26,18},{... | collective-permute-start | bytes 12296 | tf_op jit(solution)/shard_map/ppermute | solution.py:21
  66.4 35.0 %copy-start.71 = (f32[10,66]{0,1:T(8,128)}, f32[10,66]{0,1:T(8,128)S(1)}, u32[]{:S(2)}) copy-start(f32[10,66]{0,1:T(8,128)S(1)} %broadcast_multiply_fusion) | copy-start | bytes 7924
  70.7 14.8 %collective-permute-start.8 = (f32[8,66,1]{2,0,1:T(8,128)}, f32[8,66,1]{2,0,1:T(8,128)S(1)}, u32[]{:S(2)}, u32[]{:S(2)}) collective-permute-start(f32[8,66,1]{2,0,1:T(8,128)} %get-tuple-element.102), channel_id=1, source_target_pairs={{0,2},{2,4},{4,6},{1,3},{3,5},{5,7},{8,10},{10,12},{12,14},{9,11},... | collective-permute-start | bytes 6344 | tf_op jit(solution)/shard_map/ppermute | solution.py:19
  72.0 13.5 %collective-permute-start.9 = (f32[8,66,1]{2,0,1:T(8,128)}, f32[8,66,1]{2,0,1:T(8,128)S(1)}, u32[]{:S(2)}, u32[]{:S(2)}) collective-permute-start(f32[8,66,1]{2,0,1:T(8,128)} %get-tuple-element.103), channel_id=1, source_target_pairs={{2,0},{4,2},{6,4},{3,1},{5,3},{7,5},{10,8},{12,10},{14,12},{11,9},... | collective-permute-start | bytes 6344 | tf_op jit(solution)/shard_map/ppermute | solution.py:21
  77.1 12.7 %collective-permute-start.2 = (f32[2,8,68,2]{2,1,3,0:T(8,128)}, f32[2,8,68,2]{2,1,3,0:T(8,128)}, u32[]{:S(2)}, u32[]{:S(2)}) collective-permute-start(f32[2,8,68,2]{2,1,3,0:T(8,128)} %copy.24), channel_id=1, source_target_pairs={{0,2},{2,4},{4,6},{1,3},{3,5},{5,7},{8,10},{10,12},{12,14},{9,11},... | collective-permute-start | bytes 26120 | tf_op jit(solution)/shard_map/ppermute | solution.py:19
  84.2 7.5 %collective-permute-start.3 = (f32[2,8,68,2]{2,1,3,0:T(8,128)}, f32[2,8,68,2]{2,1,3,0:T(8,128)}, u32[]{:S(2)}, u32[]{:S(2)}) collective-permute-start(f32[2,8,68,2]{2,1,3,0:T(8,128)} %copy.25), channel_id=1, source_target_pairs={{2,0},{4,2},{6,4},{3,1},{5,3},{7,5},{10,8},{12,10},{14,12},{11,9},... | collective-permute-start | bytes 26120 | tf_op jit(solution)/shard_map/ppermute | solution.py:21
  86.7 14.7 %collective-permute-start.10 = (f32[1,66,130]{2,0,1:T(1,128)}, f32[1,66,130]{2,0,1:T(1,128)}, u32[]{:S(2)}, u32[]{:S(2)}) collective-permute-start(f32[1,66,130]{2,0,1:T(1,128)} %get-tuple-element.82), channel_id=1, source_target_pairs={{0,1},{2,3},{4,5},{6,7},{8,9},{10,11},{12,13},{14,15},{16,17},{18,... | collective-permute-start | bytes 102968 | tf_op jit(solution)/shard_map/ppermute | solution.py:19
  88.6 12.8 %collective-permute-start.11 = (f32[1,66,130]{2,0,1:T(1,128)}, f32[1,66,130]{2,0,1:T(1,128)}, u32[]{:S(2)}, u32[]{:S(2)}) collective-permute-start(f32[1,66,130]{2,0,1:T(1,128)} %get-tuple-element.83), channel_id=1, source_target_pairs={{1,0},{3,2},{5,4},{7,6},{9,8},{11,10},{13,12},{15,14},{17,16},{19,... | collective-permute-start | bytes 102968 | tf_op jit(solution)/shard_map/ppermute | solution.py:21
  96.1 7.9 %collective-permute-start.4 = (f32[2,2,68,132]{3,1,2,0:T(2,128)S(1)}, f32[2,2,68,132]{3,1,2,0:T(2,128)S(1)}, u32[]{:S(2)}, u32[]{:S(2)}) collective-permute-start(f32[2,2,68,132]{3,1,2,0:T(2,128)S(1)} %get-tuple-element.44), channel_id=1, source_target_pairs={{0,1},{2,3},{4,5},{6,7},{8,9},{10,11},{12,13},{14,15},{16,17},{18,... | collective-permute-start | bytes 430856 | tf_op jit(solution)/shard_map/ppermute | solution.py:19
  99.8 4.1 collective-permute-start.5
  125.3 3.5 collective-permute-start.12
  127.5 5.5 collective-permute-start.13
  133.2 10.5 %collective-permute-start.14 = (f32[8,66,1]{2,0,1:T(8,128)S(1)}, f32[8,66,1]{2,0,1:T(8,128)S(1)}, u32[]{:S(2)}, u32[]{:S(2)}) collective-permute-start(f32[8,66,1]{2,0,1:T(8,128)S(1)} %get-tuple-element.100), channel_id=1, source_target_pairs={{0,2},{2,4},{4,6},{1,3},{3,5},{5,7},{8,10},{10,12},{12,14},{9,11},... | collective-permute-start | bytes 6344 | tf_op jit(solution)/shard_map/ppermute | solution.py:19
  137.8 10.1 %collective-permute-start.15 = (f32[8,66,1]{2,0,1:T(8,128)S(1)}, f32[8,66,1]{2,0,1:T(8,128)S(1)}, u32[]{:S(2)}, u32[]{:S(2)}) collective-permute-start(f32[8,66,1]{2,0,1:T(8,128)S(1)} %get-tuple-element.101), channel_id=1, source_target_pairs={{2,0},{4,2},{6,4},{3,1},{5,3},{7,5},{10,8},{12,10},{14,12},{11,9},... | collective-permute-start | bytes 6344 | tf_op jit(solution)/shard_map/ppermute | solution.py:21
  148.3 2.7 collective-permute-start.16
  149.6 3.3 collective-permute-start.17
  202.9 34.1 %copy-start.30 = (f32[8,64,128]{2,0,1:T(8,128)}, f32[8,64,128]{2,0,1:T(8,128)S(1)}, u32[]{:S(2)}) copy-start(f32[8,64,128]{2,0,1:T(8,128)S(1)} %multiply_subtract_fusion.3) | copy-start | bytes 786436
  203.6 20.8 %collective-permute-start.18 = (f32[8,1,128]{2,0,1:T(8,128)}, f32[8,1,128]{2,0,1:T(8,128)S(1)}, u32[]{:S(2)}, u32[]{:S(2)}) collective-permute-start(f32[8,1,128]{2,0,1:T(8,128)} %get-tuple-element.114), channel_id=1, source_target_pairs={{0,8},{8,16},{16,24},{1,9},{9,17},{17,25},{2,10},{10,18},{18,26},{... | collective-permute-start | bytes 12296 | tf_op jit(solution)/shard_map/ppermute | solution.py:19
  207.8 16.6 %collective-permute-start.19 = (f32[8,1,128]{2,0,1:T(8,128)}, f32[8,1,128]{2,0,1:T(8,128)S(1)}, u32[]{:S(2)}, u32[]{:S(2)}) collective-permute-start(f32[8,1,128]{2,0,1:T(8,128)} %get-tuple-element.115), channel_id=1, source_target_pairs={{8,0},{16,8},{24,16},{9,1},{17,9},{25,17},{10,2},{18,10},{26,18},{... | collective-permute-start | bytes 12296 | tf_op jit(solution)/shard_map/ppermute | solution.py:21
  224.6 7.6 %collective-permute-start.20 = (f32[8,66,1]{2,0,1:T(8,128)S(1)}, f32[8,66,1]{2,0,1:T(8,128)S(1)}, u32[]{:S(2)}, u32[]{:S(2)}) collective-permute-start(f32[8,66,1]{2,0,1:T(8,128)S(1)} %get-tuple-element.98), channel_id=1, source_target_pairs={{0,2},{2,4},{4,6},{1,3},{3,5},{5,7},{8,10},{10,12},{12,14},{9,11},... | collective-permute-start | bytes 6344 | tf_op jit(solution)/shard_map/ppermute | solution.py:19
  228.2 8.4 %collective-permute-start.21 = (f32[8,66,1]{2,0,1:T(8,128)S(1)}, f32[8,66,1]{2,0,1:T(8,128)S(1)}, u32[]{:S(2)}, u32[]{:S(2)}) collective-permute-start(f32[8,66,1]{2,0,1:T(8,128)S(1)} %get-tuple-element.99), channel_id=1, source_target_pairs={{2,0},{4,2},{6,4},{3,1},{5,3},{7,5},{10,8},{12,10},{14,12},{11,9},... | collective-permute-start | bytes 6344 | tf_op jit(solution)/shard_map/ppermute | solution.py:21
  237.1 5.3 collective-permute-start.22
  238.4 3.9 collective-permute-start.23
  252.7 45.8 %copy-start.25 = (f32[8,64,128]{2,0,1:T(8,128)S(1)}, f32[8,64,128]{2,0,1:T(8,128)}, u32[]{:S(2)}) copy-start(f32[8,64,128]{2,0,1:T(8,128)} %copy-done.24) | copy-start | bytes 786436
  299.5 5.5 collective-permute-start.24
  303.7 5.5 collective-permute-start.25
  309.4 7.4 %collective-permute-start.26 = (f32[8,66,1]{2,0,1:T(8,128)S(1)}, f32[8,66,1]{2,0,1:T(8,128)S(1)}, u32[]{:S(2)}, u32[]{:S(2)}) collective-permute-start(f32[8,66,1]{2,0,1:T(8,128)S(1)} %get-tuple-element.96), channel_id=1, source_target_pairs={{0,2},{2,4},{4,6},{1,3},{3,5},{5,7},{8,10},{10,12},{12,14},{9,11},... | collective-permute-start | bytes 6344 | tf_op jit(solution)/shard_map/ppermute | solution.py:19
  312.8 8.4 %collective-permute-start.27 = (f32[8,66,1]{2,0,1:T(8,128)S(1)}, f32[8,66,1]{2,0,1:T(8,128)S(1)}, u32[]{:S(2)}, u32[]{:S(2)}) collective-permute-start(f32[8,66,1]{2,0,1:T(8,128)S(1)} %get-tuple-element.97), channel_id=1, source_target_pairs={{2,0},{4,2},{6,4},{3,1},{5,3},{7,5},{10,8},{12,10},{14,12},{11,9},... | collective-permute-start | bytes 6344 | tf_op jit(solution)/shard_map/ppermute | solution.py:21
  321.7 2.8 collective-permute-start.28
  323.0 3.2 collective-permute-start.29
  327.8 46.7 %copy-start.32 = (f32[8,64,128]{2,0,1:T(8,128)S(1)}, f32[8,64,128]{2,0,1:T(8,128)}, u32[]{:S(2)}) copy-start(f32[8,64,128]{2,0,1:T(8,128)} %copy-done.30) | copy-start | bytes 786436
  376.8 20.7 %collective-permute-start.30 = (f32[8,1,128]{2,0,1:T(8,128)}, f32[8,1,128]{2,0,1:T(8,128)S(1)}, u32[]{:S(2)}, u32[]{:S(2)}) collective-permute-start(f32[8,1,128]{2,0,1:T(8,128)} %get-tuple-element.110), channel_id=1, source_target_pairs={{0,8},{8,16},{16,24},{1,9},{9,17},{17,25},{2,10},{10,18},{18,26},{... | collective-permute-start | bytes 12296 | tf_op jit(solution)/shard_map/ppermute | solution.py:19
  381.1 16.4 %collective-permute-start.31 = (f32[8,1,128]{2,0,1:T(8,128)}, f32[8,1,128]{2,0,1:T(8,128)S(1)}, u32[]{:S(2)}, u32[]{:S(2)}) collective-permute-start(f32[8,1,128]{2,0,1:T(8,128)} %get-tuple-element.111), channel_id=1, source_target_pairs={{8,0},{16,8},{24,16},{9,1},{17,9},{25,17},{10,2},{18,10},{26,18},{... | collective-permute-start | bytes 12296 | tf_op jit(solution)/shard_map/ppermute | solution.py:21
  398.6 7.3 %collective-permute-start.32 = (f32[8,66,1]{2,0,1:T(8,128)S(1)}, f32[8,66,1]{2,0,1:T(8,128)S(1)}, u32[]{:S(2)}, u32[]{:S(2)}) collective-permute-start(f32[8,66,1]{2,0,1:T(8,128)S(1)} %get-tuple-element.94), channel_id=1, source_target_pairs={{0,2},{2,4},{4,6},{1,3},{3,5},{5,7},{8,10},{10,12},{12,14},{9,11},... | collective-permute-start | bytes 6344 | tf_op jit(solution)/shard_map/ppermute | solution.py:19
  401.9 8.4 %collective-permute-start.33 = (f32[8,66,1]{2,0,1:T(8,128)S(1)}, f32[8,66,1]{2,0,1:T(8,128)S(1)}, u32[]{:S(2)}, u32[]{:S(2)}) collective-permute-start(f32[8,66,1]{2,0,1:T(8,128)S(1)} %get-tuple-element.95), channel_id=1, source_target_pairs={{2,0},{4,2},{6,4},{3,1},{5,3},{7,5},{10,8},{12,10},{14,12},{11,9},... | collective-permute-start | bytes 6344 | tf_op jit(solution)/shard_map/ppermute | solution.py:21
  410.8 5.3 collective-permute-start.34
  412.1 3.9 collective-permute-start.35
  426.3 45.8 %copy-start.20 = (f32[8,64,128]{2,0,1:T(8,128)S(1)}, f32[8,64,128]{2,0,1:T(8,128)}, u32[]{:S(2)}) copy-start(f32[8,64,128]{2,0,1:T(8,128)} %copy-done.19) | copy-start | bytes 786436
  473.2 5.5 collective-permute-start.36
  477.4 5.5 collective-permute-start.37
  483.1 7.4 %collective-permute-start.38 = (f32[8,66,1]{2,0,1:T(8,128)S(1)}, f32[8,66,1]{2,0,1:T(8,128)S(1)}, u32[]{:S(2)}, u32[]{:S(2)}) collective-permute-start(f32[8,66,1]{2,0,1:T(8,128)S(1)} %get-tuple-element.92), channel_id=1, source_target_pairs={{0,2},{2,4},{4,6},{1,3},{3,5},{5,7},{8,10},{10,12},{12,14},{9,11},... | collective-permute-start | bytes 6344 | tf_op jit(solution)/shard_map/ppermute | solution.py:19
  486.5 8.4 %collective-permute-start.39 = (f32[8,66,1]{2,0,1:T(8,128)S(1)}, f32[8,66,1]{2,0,1:T(8,128)S(1)}, u32[]{:S(2)}, u32[]{:S(2)}) collective-permute-start(f32[8,66,1]{2,0,1:T(8,128)S(1)} %get-tuple-element.93), channel_id=1, source_target_pairs={{2,0},{4,2},{6,4},{3,1},{5,3},{7,5},{10,8},{12,10},{14,12},{11,9},... | collective-permute-start | bytes 6344 | tf_op jit(solution)/shard_map/ppermute | solution.py:21
  495.4 2.7 collective-permute-start.40
  496.7 3.3 collective-permute-start.41
  501.3 53.3 %copy-start.79 = (f32[256]{0:T(256)S(1)}, f32[256]{0:T(256)}, u32[]{:S(2)}) copy-start(f32[256]{0:T(256)} %copy-done.78) | copy-start | bytes 3076
  549.2 19.9 %collective-permute-start.42 = (f32[8,1,128]{2,0,1:T(8,128)}, f32[8,1,128]{2,0,1:T(8,128)S(1)}, u32[]{:S(2)}, u32[]{:S(2)}) collective-permute-start(f32[8,1,128]{2,0,1:T(8,128)} %get-tuple-element.106), channel_id=1, source_target_pairs={{0,8},{8,16},{16,24},{1,9},{9,17},{17,25},{2,10},{10,18},{18,26},{... | collective-permute-start | bytes 12296 | tf_op jit(solution)/shard_map/ppermute | solution.py:19
  553.3 15.7 %collective-permute-start.43 = (f32[8,1,128]{2,0,1:T(8,128)}, f32[8,1,128]{2,0,1:T(8,128)S(1)}, u32[]{:S(2)}, u32[]{:S(2)}) collective-permute-start(f32[8,1,128]{2,0,1:T(8,128)} %get-tuple-element.107), channel_id=1, source_target_pairs={{8,0},{16,8},{24,16},{9,1},{17,9},{25,17},{10,2},{18,10},{26,18},{... | collective-permute-start | bytes 12296 | tf_op jit(solution)/shard_map/ppermute | solution.py:21
  569.2 7.3 %collective-permute-start.44 = (f32[8,66,1]{2,0,1:T(8,128)S(1)}, f32[8,66,1]{2,0,1:T(8,128)S(1)}, u32[]{:S(2)}, u32[]{:S(2)}) collective-permute-start(f32[8,66,1]{2,0,1:T(8,128)S(1)} %get-tuple-element.90), channel_id=1, source_target_pairs={{0,2},{2,4},{4,6},{1,3},{3,5},{5,7},{8,10},{10,12},{12,14},{9,11},... | collective-permute-start | bytes 6344 | tf_op jit(solution)/shard_map/ppermute | solution.py:19
  572.5 8.4 %collective-permute-start.45 = (f32[8,66,1]{2,0,1:T(8,128)S(1)}, f32[8,66,1]{2,0,1:T(8,128)S(1)}, u32[]{:S(2)}, u32[]{:S(2)}) collective-permute-start(f32[8,66,1]{2,0,1:T(8,128)S(1)} %get-tuple-element.91), channel_id=1, source_target_pairs={{2,0},{4,2},{6,4},{3,1},{5,3},{7,5},{10,8},{12,10},{14,12},{11,9},... | collective-permute-start | bytes 6344 | tf_op jit(solution)/shard_map/ppermute | solution.py:21
  581.3 5.6 collective-permute-start.46
  582.7 4.2 collective-permute-start.47
  596.7 45.0 %copy-start.23 = (f32[8,64,128]{2,0,1:T(8,128)S(1)}, f32[8,64,128]{2,0,1:T(8,128)}, u32[]{:S(2)}) copy-start(f32[8,64,128]{2,0,1:T(8,128)} %copy-done.22) | copy-start | bytes 786436
  641.8 5.5 collective-permute-start.48
  646.0 5.5 collective-permute-start.49
  651.7 7.4 %collective-permute-start.50 = (f32[8,66,1]{2,0,1:T(8,128)S(1)}, f32[8,66,1]{2,0,1:T(8,128)S(1)}, u32[]{:S(2)}, u32[]{:S(2)}) collective-permute-start(f32[8,66,1]{2,0,1:T(8,128)S(1)} %get-tuple-element.88), channel_id=1, source_target_pairs={{0,2},{2,4},{4,6},{1,3},{3,5},{5,7},{8,10},{10,12},{12,14},{9,11},... | collective-permute-start | bytes 6344 | tf_op jit(solution)/shard_map/ppermute | solution.py:19
  655.2 8.4 %collective-permute-start.51 = (f32[8,66,1]{2,0,1:T(8,128)S(1)}, f32[8,66,1]{2,0,1:T(8,128)S(1)}, u32[]{:S(2)}, u32[]{:S(2)}) collective-permute-start(f32[8,66,1]{2,0,1:T(8,128)S(1)} %get-tuple-element.89), channel_id=1, source_target_pairs={{2,0},{4,2},{6,4},{3,1},{5,3},{7,5},{10,8},{12,10},{14,12},{11,9},... | collective-permute-start | bytes 6344 | tf_op jit(solution)/shard_map/ppermute | solution.py:21
  664.0 2.8 collective-permute-start.52
  665.3 45.3 %copy-start.21 = (f32[8,64,128]{2,0,1:T(8,128)S(1)}, f32[8,64,128]{2,0,1:T(8,128)}, u32[]{:S(2)}) copy-start(f32[8,64,128]{2,0,1:T(8,128)} %copy-done.19) | copy-start | bytes 786436
  665.3 45.3 %copy-start.26 = (f32[8,64,128]{2,0,1:T(8,128)S(1)}, f32[8,64,128]{2,0,1:T(8,128)}, u32[]{:S(2)}) copy-start(f32[8,64,128]{2,0,1:T(8,128)} %copy-done.24) | copy-start | bytes 786436
  665.3 3.3 collective-permute-start.53
  (76 other events, 843.7 us)
